TPU v7x, 32 devices: a whole 2x2x4 slice. The times are simulated.
32 devices in a mesh: groups: 2 (over x), rows: 16 (over z, y, core).
Axes of the slice: x: 2, y: 2, z: 4, core: 2. Of those that a mesh axis runs over, the one named last changes fastest.
Arguments:
- block_input: bfloat16 [512, 352, 512], P(('groups', 'rows')), parts along dimension 0, may hold values from -6 to 6
- first_pre: bfloat16 [512, 352, 128], P(('groups', 'rows')), parts along dimension 0, may hold values from -6 to 6
- second_pre: bfloat16 [512, 352, 128], P(('groups', 'rows')), parts along dimension 0, may hold values from -6 to 6
- output_pre: bfloat16 [512, 352, 512], P(('groups', 'rows')), parts along dimension 0, may hold values from -6 to 6
- output_grad: bfloat16 [512, 352, 512], P('groups', None, 'rows'), parts along dimension 0, may hold values from -6 to 6
- first_weight: bfloat16 [512, 128], replicated, may hold values from -0.25 to 0.25
- middle_weight: bfloat16 [3, 3, 128, 128], replicated, may hold values from -0.1875 to 0.1875
- last_weight: bfloat16 [128, 512], replicated, may hold values from -0.5 to 0.5
Outputs:
- input_grad: bfloat16 [512, 352, 512], P(('groups', 'rows')), parts along dimension 0
- first_weight_grad: float32 [1024, 128], P(('groups', 'rows')), parts along dimension 0
- middle_weight_grad: float32 [6, 3, 128, 128], P('groups'), parts along dimension 0
- last_weight_grad: float32 [256, 512], P('groups'), parts along dimension 0
There are 2 independent parts, one for each index of `groups`. A program takes and returns all parts, laid end to end along the dimension named above; an argument that names none is the same for every part. Nothing has to cross between parts.
All inputs are finite; a program needn't handle non-finite values.
Results may differ from a plain program's by a relative error of at most 0.0049.
Values may be sent and summed in bfloat16 or wider, within the bound.
No kernel may reach another device: no remote copies, remote signals or barrier semaphores. Data moves between devices by JAX's collectives and lax.ppermute only.
A program may use at most 128 MiB of HBM per device.

v0:
```python
import math
import jax
import jax.numpy as jnp
from jax import lax
from jax.sharding import PartitionSpec as P


def with_halo(value, sides, width):
    for axis, dim in sides:
        size, length = (lax.axis_size(axis), value.shape[dim])
        up = [(i, (i + 1) % size) for i in range(size - 1)]
        down = [(j, i) for i, j in up]
        last = lax.slice_in_dim(value, length - width, length, axis=dim)
        leading = lax.slice_in_dim(value, 0, width, axis=dim)
        before = lax.ppermute(last, axis, up)
        after = lax.ppermute(leading, axis, down)
        value = jnp.concatenate([before, value, after], axis=dim)
    return value


def contract_rows(left, right):
    return lax.dot_general(
        left, right, (((0,), (0,)), ((), ())), preferred_element_type=jnp.float32
    )


def shards(
    block_input,
    first_pre,
    second_pre,
    output_pre,
    output_grad,
    first_weight,
    middle_weight,
    last_weight,
):
    tile_rows, map_cols, channels = block_input.shape
    inner_width = first_pre.shape[2]
    pixels = tile_rows * map_cols
    factor = 1.0 / math.sqrt(pixels * lax.axis_size("rows"))
    spatial = lax.all_to_all(output_grad, "rows", split_axis=0, concat_axis=2, tiled=True)
    masked_out = jnp.where(output_pre > 0, spatial, jnp.zeros_like(spatial))
    second_act = jnp.maximum(second_pre, jnp.zeros_like(second_pre))
    first_act = jnp.maximum(first_pre, jnp.zeros_like(first_pre))
    out_flat = masked_out.reshape(pixels, channels)
    last_part = contract_rows(second_act.reshape(pixels, inner_width), out_flat)
    last_total = lax.psum(last_part, "rows")
    inner = lax.dot_general(
        out_flat, last_weight, (((1,), (1,)), ((), ())), preferred_element_type=jnp.float32
    )
    second_grad = jnp.where(second_pre.reshape(pixels, inner_width) > 0, inner, 0.0).astype(
        jnp.bfloat16
    )
    second_flat = second_grad
    second_grad = second_flat.reshape(tile_rows, map_cols, inner_width)
    act_ext = with_halo(first_act, (("rows", 0),), 1)
    act_padded = jnp.pad(act_ext, ((0, 0), (1, 1), (0, 0)))
    taps = []
    for row_tap in range(3):
        line = []
        for col_tap in range(3):
            window = act_padded[
                row_tap : row_tap + tile_rows, col_tap : col_tap + map_cols
            ].reshape(pixels, inner_width)
            line.append(contract_rows(window, second_flat))
        taps.append(jnp.stack(line))
    middle_part = jnp.stack(taps)
    grad_ext = with_halo(second_grad, (("rows", 0),), 1)
    grad_padded = jnp.pad(grad_ext, ((0, 0), (1, 1), (0, 0)))
    total = jnp.zeros((pixels, inner_width), jnp.float32)
    for row_tap in range(3):
        for col_tap in range(3):
            moved = grad_padded[
                2 - row_tap : 2 - row_tap + tile_rows, 2 - col_tap : 2 - col_tap + map_cols
            ].reshape(pixels, inner_width)
            total = total + lax.dot_general(
                moved,
                middle_weight[row_tap, col_tap],
                (((1,), (1,)), ((), ())),
                preferred_element_type=jnp.float32,
            )
    first_grad = jnp.where(first_pre.reshape(pixels, inner_width) > 0, total, 0.0).astype(
        jnp.bfloat16
    )
    input_flat = block_input.reshape(pixels, channels)
    first_wgrad = (
        lax.psum_scatter(
            contract_rows(input_flat, first_grad), "rows", scatter_dimension=0, tiled=True
        )
        * factor
    )
    back = lax.dot_general(
        first_grad, first_weight, (((1,), (1,)), ((), ())), preferred_element_type=jnp.float32
    )
    input_grad = (
        (back + out_flat.astype(jnp.float32))
        .astype(jnp.bfloat16)
        .reshape(tile_rows, map_cols, channels)
    )
    middle_total = lax.psum(middle_part, "rows")
    return (input_grad, first_wgrad, middle_total * factor, last_total * factor)


def solution(mesh):
    placed = (
        P(("groups", "rows"), None, None),
        P(("groups", "rows"), None, None),
        P(("groups", "rows"), None, None),
        P(("groups", "rows"), None, None),
        P("groups", None, "rows"),
        P(),
        P(),
        P(),
    )
    return jax.shard_map(
        shards,
        mesh=mesh,
        in_specs=placed,
        out_specs=(
            P(("groups", "rows"), None, None),
            P(("groups", "rows"), None),
            P("groups", None, None, None),
            P("groups", None),
        ),
        check_vma=False,
    )
```

profile of v0, /device:TPU:0, one launch (start us, length us, event | category | flops | bytes accessed | tf_op | source)
XLA Modules:
  0.0 376.6 jit_solution(985985323894171516)
XLA Ops:
  7.2 9.7 %copy.21 = bf16[256,352,32]{1,2,0:T(8,128)(2,1)} copy(bf16[256,352,32]{0,2,1:T(8,128)(2,1)} %param.12) | data formatting | bytes 11534336 | tf_op args[4]
  16.8 7.6 %all-to-all-start = ((bf16[256,352,32]{1,2,0:T(8,128)(2,1)}), bf16[256,352,32]{1,2,0:T(8,128)(2,1)}, u32[]{:S(2)}, u32[]{:S(2)}) async-start(bf16[256,352,32]{1,2,0:T(8,128)(2,1)} %copy.21), calls=%async_computation | async-start | bytes 12582912 | tf_op jit(solution)/shard_map/all_to_all | solution.py:41
  24.6 2.4 collective-permute-start.2
  27.0 1.3 collective-permute-start.3
  28.3 1.3 broadcast_compare_fusion.1
  29.6 1.3 broadcast_compare_fusion
  30.9 8.3 %copy.20 = bf16[16,352,512]{1,2,0:T(8,128)(2,1)} copy(bf16[16,352,512]{2,1,0:T(8,128)(2,1)} %param.11) | data formatting | bytes 11534336 | tf_op args[3]
  39.2 1.7 pad_maximum_fusion.1
  41.4 3.9 %fusion.33 = (bf16[16,352,128]{2,1,0:T(8,128)(2,1)}, bf16[16,352,128]{2,1,0:T(8,128)(2,1)}, bf16[16,352,128]{2,1,0:T(8,128)(2,1)}, bf16[16,352,128]{2,1,0:T(8,12...) fusion(bf16[18,354,128]{2,1,0:T(8,128)(2,1)S(1)} %select_maximum_fusion), kind=kLoop, calls=%fused_computation.73 | loop fusion | bytes 17301504 | tf_op jit(solution)/shard_map/slice | solution.py:62
  45.3 93.3 %all-to-all-done = bf16[256,352,32]{1,2,0:T(8,128)(2,1)} async-done(((bf16[256,352,32]{1,2,0:T(8,128)(2,1)}), bf16[256,352,32]{1,2,0:T(8,128)(2,1)}, u32[]{:S(2)}, u32[]{:S(2)}) %all-to-all-start) | async-done | bytes 5767200 | tf_op jit(solution)/shard_map/all_to_all | solution.py:41
  138.6 6.4 %copy.22 = bf16[16,352,16,32]{1,3,2,0:T(8,128)(2,1)} copy(bf16[16,352,16,32]{1,3,0,2:T(8,128)(2,1)} %bitcast.3) | data formatting | bytes 11534336 | tf_op jit(solution)/shard_map/all_to_all | solution.py:41
  145.0 8.0 %compare_select_fusion = bf16[16,352,512]{1,2,0:T(8,128)(2,1)} fusion(bf16[16,352,512]{1,2,0:T(8,128)(2,1)} %copy.20, bf16[16,352,16,32]{1,3,2,0:T(8,128)(2,1)} %copy.22), kind=kLoop, calls=%fused_computation | loop fusion | flops 5767168 | bytes 17301504 | tf_op jit(solution)/shard_map/jit(_where)/select_n | solution.py:42
  153.1 8.5 %copy.23 = bf16[16,352,512]{2,1,0:T(8,128)(2,1)} copy(bf16[16,352,512]{1,2,0:T(8,128)(2,1)} %compare_select_fusion) | data formatting | bytes 11534336 | tf_op jit(solution)/shard_map/jit(_where)/select_n | solution.py:42
  161.6 5.8 %fusion.8 = f32[128,512]{1,0:T(8,128)} fusion(bf16[16,352,512]{1,2,0:T(8,128)(2,1)} %compare_select_fusion, bf16[16,352,128]{2,1,0:T(8,128)(2,1)S(1)} %copy-done.12), kind=kOutput, calls=%fused_computation.28 | convolution fusion | flops 738918400 | bytes 7471104 | tf_op jit(solution)/shard_map/dot_general | solution.py:22
  167.5 1.7 fusion.3
  179.9 2.7 collective-permute-start
  182.6 1.3 collective-permute-start.1
  185.0 8.5 %collective-permute-done.1 = bf16[1,352,128]{2,1,0:T(8,128)(2,1)S(1)} collective-permute-done((bf16[1,352,128]{2,1,0:T(8,128)(2,1)S(1)}, bf16[1,352,128]{2,1,0:T(8,128)(2,1)S(1)}, u32[]{:S(2)}, u32[]{:S(2)}) %collective-permute-start.1) | collective-permute-done | bytes 90144 | tf_op jit(solution)/shard_map/ppermute | solution.py:16
  194.1 2.4 fusion.34
  205.5 6.8 %add_convert_fusion = bf16[5632,512]{1,0:T(8,128)(2,1)} fusion(bf16[5632,512]{1,0:T(8,128)(2,1)} %bitcast.124, bf16[5632,128]{1,0:T(8,128)(2,1)S(1)} %fusion.2, bf16[512,128]{1,0:T(8,128)(2,1)S(1)} %copy-done), kind=kOutput, calls=%fused_computation.1 | convolution fusion | flops 746848256 | bytes 13107200 | tf_op jit(solution)/shard_map/dot_general | solution.py:92
  212.3 97.3 %all-reduce.5.cloned.1.call-done = (f32[3,3,128,128]{3,2,1,0:T(8,128)}, f32[128,512]{1,0:T(8,128)}) async-done(((f32[3,3,128,128]{3,2,1,0:T(8,128)}, f32[128,512]{1,0:T(8,128)}), (f32[3,3,128,128]{3,2,1,0:T(8,128)}, f32[128,512]{1,0:T(8,128)})) %all-reduce.5.cloned.1.call-update) | async-done | bytes 851984 | tf_op jit(solution)/shard_map/psum | solution.py:100
  309.6 1.7 broadcast_multiply_fusion.1
  311.3 1.9 broadcast_multiply_fusion
  313.2 55.1 %reduce-scatter.4.cloned.1.call-done = f32[32,128]{1,0:T(8,128)} async-done(((f32[512,128]{1,0:T(8,128)}), f32[32,128]{1,0:T(8,128)}) %reduce-scatter.4.cloned.1.call-update) | async-done | bytes 16400
  (78 shorter events, 23.3 us)
Async XLA Ops:
  7.2 198.3 %copy-start = (bf16[512,128]{1,0:T(8,128)(2,1)S(1)}, bf16[512,128]{1,0:T(8,128)(2,1)}, u32[]{:S(2)}) copy-start(bf16[512,128]{1,0:T(8,128)(2,1)} %param.13) | copy-start | bytes 393220
  16.8 7.6 %copy-start.2 = (bf16[16,352,128]{2,1,0:T(8,128)(2,1)S(1)}, bf16[16,352,128]{2,1,0:T(8,128)(2,1)}, u32[]{:S(2)}) copy-start(bf16[16,352,128]{2,1,0:T(8,128)(2,1)} %param.9) | copy-start | bytes 4325380
  16.8 121.8 %all-to-all-start = ((bf16[256,352,32]{1,2,0:T(8,128)(2,1)}), bf16[256,352,32]{1,2,0:T(8,128)(2,1)}, u32[]{:S(2)}, u32[]{:S(2)}) async-start(bf16[256,352,32]{1,2,0:T(8,128)(2,1)} %copy.21), calls=%async_computation | async-start | bytes 12582912 | tf_op jit(solution)/shard_map/all_to_all | solution.py:41
  24.4 285.2 %all-reduce.5.cloned.1.call-start = ((), (), s32[]{:S(2)}) async-start(), calls=%async_computation.3 | async-start | bytes 1703936 | tf_op jit(solution)/shard_map/psum | solution.py:100
  24.6 5.0 %copy-start.11 = (bf16[16,352,128]{2,1,0:T(8,128)(2,1)S(1)}, bf16[16,352,128]{2,1,0:T(8,128)(2,1)}, u32[]{:S(2)}) copy-start(bf16[16,352,128]{2,1,0:T(8,128)(2,1)} %param.10) | copy-start | bytes 4325380
  24.6 14.6 %collective-permute-start.2 = (bf16[1,352,128]{2,1,0:T(8,128)(2,1)S(1)}, bf16[1,352,128]{2,1,0:T(8,128)(2,1)S(1)}, u32[]{:S(2)}, u32[]{:S(2)}) collective-permute-start(bf16[1,352,128]{2,1,0:T(8,128)(2,1)S(1)} %get-tuple-element.32), channel_id=1, source_target_pairs={{0,1},{1,2},{2,3},{3,4},{4,5},{5,6},{6,7},{7,8},{8,9},{9,10},{10,1... | collective-permute-start | bytes 270344 | tf_op jit(solution)/shard_map/ppermute | solution.py:15
  27.0 12.2 %collective-permute-start.3 = (bf16[1,352,128]{2,1,0:T(8,128)(2,1)S(1)}, bf16[1,352,128]{2,1,0:T(8,128)(2,1)S(1)}, u32[]{:S(2)}, u32[]{:S(2)}) collective-permute-start(bf16[1,352,128]{2,1,0:T(8,128)(2,1)S(1)} %get-tuple-element.33), channel_id=1, source_target_pairs={{1,0},{2,1},{3,2},{4,3},{5,4},{6,5},{7,6},{8,7},{9,8},{10,9},{11,1... | collective-permute-start | bytes 270344 | tf_op jit(solution)/shard_map/ppermute | solution.py:16
  153.1 8.5 %copy-start.12 = (bf16[16,352,128]{2,1,0:T(8,128)(2,1)S(1)}, bf16[16,352,128]{2,1,0:T(8,128)(2,1)}, u32[]{:S(2)}) copy-start(bf16[16,352,128]{2,1,0:T(8,128)(2,1)} %param.10) | copy-start | bytes 4325380
  161.6 5.8 %copy-start.1 = (bf16[16,352,512]{2,1,0:T(8,128)(2,1)S(1)}, bf16[16,352,512]{2,1,0:T(8,128)(2,1)}, u32[]{:S(2)}) copy-start(bf16[16,352,512]{2,1,0:T(8,128)(2,1)} %copy.23) | copy-start | bytes 17301508
  161.6 5.8 %copy-start.14 = (pred[16,352,128]{2,1,0:T(32,128)(4,1)S(1)}, pred[16,352,128]{2,1,0:T(32,128)(4,1)}, u32[]{:S(2)}) copy-start(pred[16,352,128]{2,1,0:T(32,128)(4,1)} %broadcast_compare_fusion) | copy-start | bytes 2162692
  161.6 5.8 %copy-start.16 = (bf16[128,512]{1,0:T(8,128)(2,1)S(1)}, bf16[128,512]{1,0:T(8,128)(2,1)}, u32[]{:S(2)}) copy-start(bf16[128,512]{1,0:T(8,128)(2,1)} %param.15) | copy-start | bytes 393220
  167.5 1.7 copy-start.10
  169.2 1.4 copy-start.9
  170.5 1.4 copy-start.8
  171.9 1.4 copy-start.7
  173.3 1.4 copy-start.4
  175.2 1.4 copy-start.6
  176.6 1.4 copy-start.5
  179.9 5.2 %collective-permute-start = (bf16[1,352,128]{2,1,0:T(8,128)(2,1)S(1)}, bf16[1,352,128]{2,1,0:T(8,128)(2,1)S(1)}, u32[]{:S(2)}, u32[]{:S(2)}) collective-permute-start(bf16[1,352,128]{2,1,0:T(8,128)(2,1)S(1)} %get-tuple-element.36), channel_id=1, source_target_pairs={{0,1},{1,2},{2,3},{3,4},{4,5},{5,6},{6,7},{7,8},{8,9},{9,10},{10,1... | collective-permute-start | bytes 270344 | tf_op jit(solution)/shard_map/ppermute | solution.py:15
  182.6 11.0 %collective-permute-start.1 = (bf16[1,352,128]{2,1,0:T(8,128)(2,1)S(1)}, bf16[1,352,128]{2,1,0:T(8,128)(2,1)S(1)}, u32[]{:S(2)}, u32[]{:S(2)}) collective-permute-start(bf16[1,352,128]{2,1,0:T(8,128)(2,1)S(1)} %get-tuple-element.37), channel_id=1, source_target_pairs={{1,0},{2,1},{3,2},{4,3},{5,4},{6,5},{7,6},{8,7},{9,8},{10,9},{11,1... | collective-permute-start | bytes 270344 | tf_op jit(solution)/shard_map/ppermute | solution.py:16
  184.8 183.4 %reduce-scatter.4.cloned.1.call-start = ((), (), s32[]{:S(2)}) async-start(), calls=%async_computation.2 | async-start | bytes 278528
  194.1 2.4 copy-start.15
  200.5 2.4 slice-start
  201.6 2.0 slice-start.1
  (2 other events, 2.5 us)
Sparse Core Ops, SparseCore 0:
  184.9 124.6 all-reduce.4
  313.1 55.1 reduce-scatter.3
where the time goes:
time: 378 us; the launch traced here: 377 us
  waiting for transfers between devices  254 us (67%)
  local copies, waits for them, and re-layouts  48.8 us (13%)
  matrix products  25.6 us (7%)
  other arithmetic  18 us (5%)
  starting transfers between devices  15.5 us (4%)
  between operations  14.4 us (4%)
    psum x1, waiting for transfers between devices, shards(): middle_total = lax.psum(middle_part, 'rows')  97.3 us
    all_to_all x1, waiting for transfers between devices, shards(): lax.all_to_all(output_grad, 'rows', split_axis=0, concat_axis=2, tiled=True)  93.3 us
    unnamed x3, waiting for transfers between devices  55.1 us
    unnamed x43, local copies, waits for them, and re-layouts  27.6 us
    dot_general x11, matrix products, contract_rows(): lax.dot_general(left, right, (((0,), (0,)), ((), ())), preferred_element_...  12 us
    ppermute x2, waiting for transfers between devices, with_halo(): after = lax.ppermute(leading, axis, down)  8.54 us
    select_n x1, local copies, waits for them, and re-layouts, shards(): masked_out = jnp.where(output_pre > 0, spatial, jnp.zeros_like(spatial))  8.53 us
    select_n x1, other arithmetic, shards(): masked_out = jnp.where(output_pre > 0, spatial, jnp.zeros_like(spatial))  8.04 us
  transfers between devices with their start and end apart: 7, of which 4 were waited for; matrix products, arithmetic and copies ran while one was open for 10% of the time, Pallas kernels for 0%

commit v1 on v0

--- a/solution.py
+++ b/solution.py
@@ -3,6 +3,12 @@
 import jax.numpy as jnp
 from jax import lax
 from jax.sharding import PartitionSpec as P
+
+
+def swap_blocks(shard, name, split, join):
+    parts = jnp.split(shard, lax.axis_size(name), axis=split)
+    arrived = lax.all_to_all(jnp.stack(parts), name, 0, 0)
+    return jnp.concatenate(arrived, axis=join)
 
 
 def with_halo(value, sides, width):
@@ -38,7 +44,7 @@
     inner_width = first_pre.shape[2]
     pixels = tile_rows * map_cols
     factor = 1.0 / math.sqrt(pixels * lax.axis_size("rows"))
-    spatial = lax.all_to_all(output_grad, "rows", split_axis=0, concat_axis=2, tiled=True)
+    spatial = swap_blocks(output_grad, "rows", 0, 2)
     masked_out = jnp.where(output_pre > 0, spatial, jnp.zeros_like(spatial))
     second_act = jnp.maximum(second_pre, jnp.zeros_like(second_pre))
     first_act = jnp.maximum(first_pre, jnp.zeros_like(first_pre))

time: 378 us -> 507 us (1.34); the launches traced: 377 us -> 497 us
  local copies, waits for them, and re-layouts: 48.8 us -> 171 us
    unnamed x43 -> x101, local copies, waits for them, and re-layouts: 27.6 us -> 121 us
    split x0 -> x1, local copies, waits for them, and re-layouts: none -> 30.5 us  [swap_blocks(): parts = jnp.split(shard, lax.axis_size(name), axis=split)]
    all_to_all x1 -> x0, local copies, waits for them, and re-layouts: 6.43 us -> none  [shards(): lax.all_to_all(output_grad, 'rows', split_axis=0, concat_axis=2, tiled=True)]
  transfers between devices with their start and end apart: 7 -> 7, of which waited for: 4 -> 4; matrix products, arithmetic and copies ran while one was open for 10% -> 8% of each run, Pallas kernels for 0% -> 0%
where the time goes in v1:
time: 507 us; the launch traced here: 497 us
  waiting for transfers between devices  254 us (50%)
  local copies, waits for them, and re-layouts  171 us (34%)
  matrix products  25.6 us (5%)
  other arithmetic  16.3 us (3%)
  starting transfers between devices  15.4 us (3%)
  between operations  14.7 us (3%)
    unnamed x101, local copies, waits for them, and re-layouts  121 us
    psum x1, waiting for transfers between devices, shards(): middle_total = lax.psum(middle_part, 'rows')  97.2 us
    all_to_all x1, waiting for transfers between devices, swap_blocks(): arrived = lax.all_to_all(jnp.stack(parts), name, 0, 0)  93 us
    unnamed x3, waiting for transfers between devices  55.1 us
    split x1, local copies, waits for them, and re-layouts, swap_blocks(): parts = jnp.split(shard, lax.axis_size(name), axis=split)  30.5 us
    dot_general x11, matrix products, contract_rows(): lax.dot_general(left, right, (((0,), (0,)), ((), ())), preferred_element_...  12 us
  transfers between devices with their start and end apart: 7, of which 4 were waited for; matrix products, arithmetic and copies ran while one was open for 8% of the time, Pallas kernels for 0%

profile of v1, /device:TPU:0, one launch (start us, length us, event | category | flops | bytes accessed | tf_op | source)
XLA Modules:
  0.0 497.2 jit_solution(3860013397703689160)
XLA Ops:
  7.2 30.5 %fusion.33 = (bf16[16,352,32]{0,2,1:T(8,128)(2,1)S(1)}, bf16[16,352,32]{0,2,1:T(8,128)(2,1)}, bf16[16,352,32]{0,2,1:T(8,128)(2,1)}, bf16[16,352,32]{0,2,1:T(8,12...) fusion(bf16[256,352,32]{0,2,1:T(8,128)(2,1)} %param.12), kind=kLoop, calls=%fused_computation.89 | loop fusion | bytes 11534336 | tf_op jit(solution)/shard_map/split | solution.py:9
  43.7 5.8 %copy.43 = bf16[16,352,32]{1,2,0:T(8,128)(2,1)} copy(bf16[16,352,32]{0,2,1:T(8,128)(2,1)} %get-tuple-element.32) | data formatting | bytes 720896
  49.4 5.8 %copy.44 = bf16[16,352,32]{1,2,0:T(8,128)(2,1)} copy(bf16[16,352,32]{0,2,1:T(8,128)(2,1)} %get-tuple-element.31) | data formatting | bytes 720896
  55.2 5.8 %copy.45 = bf16[16,352,32]{1,2,0:T(8,128)(2,1)} copy(bf16[16,352,32]{0,2,1:T(8,128)(2,1)} %get-tuple-element.30) | data formatting | bytes 720896
  61.0 5.8 %copy.46 = bf16[16,352,32]{1,2,0:T(8,128)(2,1)} copy(bf16[16,352,32]{0,2,1:T(8,128)(2,1)} %get-tuple-element.29) | data formatting | bytes 720896
  66.8 5.8 %copy.47 = bf16[16,352,32]{1,2,0:T(8,128)(2,1)} copy(bf16[16,352,32]{0,2,1:T(8,128)(2,1)} %get-tuple-element.28) | data formatting | bytes 720896
  72.6 6.0 %copy.48 = bf16[16,352,32]{1,2,0:T(8,128)(2,1)} copy(bf16[16,352,32]{0,2,1:T(8,128)(2,1)} %get-tuple-element.27) | data formatting | bytes 720896
  78.5 5.8 %copy.49 = bf16[16,352,32]{1,2,0:T(8,128)(2,1)} copy(bf16[16,352,32]{0,2,1:T(8,128)(2,1)} %get-tuple-element.26) | data formatting | bytes 720896
  84.3 5.8 %copy.50 = bf16[16,352,32]{1,2,0:T(8,128)(2,1)} copy(bf16[16,352,32]{0,2,1:T(8,128)(2,1)} %get-tuple-element.25) | data formatting | bytes 720896
  90.1 5.8 %copy.51 = bf16[16,352,32]{1,2,0:T(8,128)(2,1)} copy(bf16[16,352,32]{0,2,1:T(8,128)(2,1)} %get-tuple-element.24) | data formatting | bytes 720896
  95.9 5.8 %copy.52 = bf16[16,352,32]{1,2,0:T(8,128)(2,1)} copy(bf16[16,352,32]{0,2,1:T(8,128)(2,1)} %get-tuple-element.23) | data formatting | bytes 720896
  101.6 5.8 %copy.53 = bf16[16,352,32]{1,2,0:T(8,128)(2,1)} copy(bf16[16,352,32]{0,2,1:T(8,128)(2,1)} %get-tuple-element.22) | data formatting | bytes 720896
  107.4 5.8 %copy.54 = bf16[16,352,32]{1,2,0:T(8,128)(2,1)} copy(bf16[16,352,32]{0,2,1:T(8,128)(2,1)} %get-tuple-element.21) | data formatting | bytes 720896
  113.2 5.8 %copy.55 = bf16[16,352,32]{1,2,0:T(8,128)(2,1)} copy(bf16[16,352,32]{0,2,1:T(8,128)(2,1)} %get-tuple-element.20) | data formatting | bytes 720896
  143.2 7.6 %all-to-all-start = ((bf16[16,16,352,32]{2,3,1,0:T(8,128)(2,1)}), bf16[16,16,352,32]{2,3,1,0:T(8,128)(2,1)}, u32[]{:S(2)}, u32[]{:S(2)}) async-start(bf16[16,16,352,32]{2,3,1,0:T(8,128)(2,1)} %bitcast_dynamic-update-slice_fusion), calls=%async_computation | async-start | bytes 12582912 | tf_op jit(solution)/shard_map/all_to_all | solution.py:10
  157.4 8.4 %copy.18 = bf16[16,352,512]{1,2,0:T(8,128)(2,1)} copy(bf16[16,352,512]{2,1,0:T(8,128)(2,1)} %param.11) | data formatting | bytes 11534336 | tf_op args[3]
  172.0 93.0 %all-to-all-done = bf16[16,16,352,32]{2,3,1,0:T(8,128)(2,1)} async-done(((bf16[16,16,352,32]{2,3,1,0:T(8,128)(2,1)}), bf16[16,16,352,32]{2,3,1,0:T(8,128)(2,1)}, u32[]{:S(2)}, u32[]{:S(2)}) %all-to-all-start) | async-done | bytes 5767200 | tf_op jit(solution)/shard_map/all_to_all | solution.py:10
  268.7 6.2 %compare_select_fusion = bf16[16,352,512]{1,2,0:T(8,128)(2,1)} fusion(bf16[16,352,512]{1,2,0:T(8,128)(2,1)} %copy.18, bf16[16,352,16,32]{1,3,2,0:T(8,128)(2,1)S(1)} %copy.35), kind=kLoop, calls=%fused_computation | loop fusion | flops 5767168 | bytes 17301504 | tf_op jit(solution)/shard_map/jit(_where)/select_n | solution.py:48
  274.9 8.9 %copy.36 = bf16[16,352,512]{2,1,0:T(8,128)(2,1)} copy(bf16[16,352,512]{1,2,0:T(8,128)(2,1)} %compare_select_fusion) | data formatting | bytes 11534336 | tf_op jit(solution)/shard_map/jit(_where)/select_n | solution.py:48
  283.9 5.8 %fusion.8 = f32[128,512]{1,0:T(8,128)} fusion(bf16[16,352,512]{1,2,0:T(8,128)(2,1)} %compare_select_fusion, bf16[16,352,128]{2,1,0:T(8,128)(2,1)S(1)} %copy-done.14), kind=kOutput, calls=%fused_computation.28 | convolution fusion | flops 738918400 | bytes 7471104 | tf_op jit(solution)/shard_map/dot_general | solution.py:28
  305.3 8.7 %collective-permute-done.1 = bf16[1,352,128]{2,1,0:T(8,128)(2,1)S(1)} collective-permute-done((bf16[1,352,128]{2,1,0:T(8,128)(2,1)S(1)}, bf16[1,352,128]{2,1,0:T(8,128)(2,1)S(1)}, u32[]{:S(2)}, u32[]{:S(2)}) %collective-permute-start.1) | collective-permute-done | bytes 90144 | tf_op jit(solution)/shard_map/ppermute | solution.py:22
  326.0 6.8 %add_convert_fusion = bf16[5632,512]{1,0:T(8,128)(2,1)} fusion(bf16[5632,512]{1,0:T(8,128)(2,1)} %bitcast.154, bf16[5632,128]{1,0:T(8,128)(2,1)S(1)} %fusion.2, bf16[512,128]{1,0:T(8,128)(2,1)S(1)} %copy-done), kind=kOutput, calls=%fused_computation.1 | convolution fusion | flops 746848256 | bytes 13107200 | tf_op jit(solution)/shard_map/dot_general | solution.py:98
  332.9 97.2 %all-reduce.5.cloned.1.call-done = (f32[3,3,128,128]{3,2,1,0:T(8,128)}, f32[128,512]{1,0:T(8,128)}) async-done(((f32[3,3,128,128]{3,2,1,0:T(8,128)}, f32[128,512]{1,0:T(8,128)}), (f32[3,3,128,128]{3,2,1,0:T(8,128)}, f32[128,512]{1,0:T(8,128)})) %all-reduce.5.cloned.1.call-update) | async-done | bytes 851984 | tf_op jit(solution)/shard_map/psum | solution.py:106
  433.6 55.1 %reduce-scatter.4.cloned.1.call-done = f32[32,128]{1,0:T(8,128)} async-done(((f32[512,128]{1,0:T(8,128)}), f32[32,128]{1,0:T(8,128)}) %reduce-scatter.4.cloned.1.call-update) | async-done | bytes 16400
  (138 shorter events, 78.9 us)
Async XLA Ops:
  7.2 318.8 %copy-start = (bf16[512,128]{1,0:T(8,128)(2,1)S(1)}, bf16[512,128]{1,0:T(8,128)(2,1)}, u32[]{:S(2)}) copy-start(bf16[512,128]{1,0:T(8,128)(2,1)} %param.13) | copy-start | bytes 393220
  129.0 3.7 copy-start.28
  129.0 4.6 copy-start.27
  129.0 5.4 %copy-start.26 = (bf16[16,352,32]{1,2,0:T(8,128)(2,1)S(1)}, bf16[16,352,32]{1,2,0:T(8,128)(2,1)}, u32[]{:S(2)}) copy-start(bf16[16,352,32]{1,2,0:T(8,128)(2,1)} %copy.47) | copy-start | bytes 1081348
  130.9 4.3 copy-start.25
  132.7 3.2 copy-start.24
  134.4 3.2 copy-start.22
  136.0 3.2 copy-start.20
  136.8 3.2 copy-start.19
  137.6 3.2 copy-start.18
  143.2 7.6 %copy-start.4 = (bf16[16,352,128]{2,1,0:T(8,128)(2,1)S(1)}, bf16[16,352,128]{2,1,0:T(8,128)(2,1)}, u32[]{:S(2)}) copy-start(bf16[16,352,128]{2,1,0:T(8,128)(2,1)} %param.9) | copy-start | bytes 4325380
  143.2 121.8 %all-to-all-start = ((bf16[16,16,352,32]{2,3,1,0:T(8,128)(2,1)}), bf16[16,16,352,32]{2,3,1,0:T(8,128)(2,1)}, u32[]{:S(2)}, u32[]{:S(2)}) async-start(bf16[16,16,352,32]{2,3,1,0:T(8,128)(2,1)} %bitcast_dynamic-update-slice_fusion), calls=%async_computation | async-start | bytes 12582912 | tf_op jit(solution)/shard_map/all_to_all | solution.py:10
  150.7 279.3 %all-reduce.5.cloned.1.call-start = ((), (), s32[]{:S(2)}) async-start(), calls=%async_computation.3 | async-start | bytes 1703936 | tf_op jit(solution)/shard_map/psum | solution.py:106
  150.9 16.7 %copy-start.2 = (bf16[16,352,128]{2,1,0:T(8,128)(2,1)}, bf16[16,352,128]{2,1,0:T(8,128)(2,1)S(1)}, u32[]{:S(2)}) copy-start(bf16[16,352,128]{2,1,0:T(8,128)(2,1)S(1)} %broadcast_maximum_fusion) | copy-start | bytes 4325380
  150.9 5.2 %copy-start.13 = (bf16[16,352,128]{2,1,0:T(8,128)(2,1)S(1)}, bf16[16,352,128]{2,1,0:T(8,128)(2,1)}, u32[]{:S(2)}) copy-start(bf16[16,352,128]{2,1,0:T(8,128)(2,1)} %param.10) | copy-start | bytes 4325380
  150.9 14.9 %collective-permute-start.2 = (bf16[1,352,128]{2,1,0:T(8,128)(2,1)S(1)}, bf16[1,352,128]{2,1,0:T(8,128)(2,1)S(1)}, u32[]{:S(2)}, u32[]{:S(2)}) collective-permute-start(bf16[1,352,128]{2,1,0:T(8,128)(2,1)S(1)} %get-tuple-element.48), channel_id=1, source_target_pairs={{0,1},{1,2},{2,3},{3,4},{4,5},{5,6},{6,7},{7,8},{8,9},{9,10},{10,1... | collective-permute-start | bytes 270344 | tf_op jit(solution)/shard_map/ppermute | solution.py:21
  153.5 12.3 %collective-permute-start.3 = (bf16[1,352,128]{2,1,0:T(8,128)(2,1)S(1)}, bf16[1,352,128]{2,1,0:T(8,128)(2,1)S(1)}, u32[]{:S(2)}, u32[]{:S(2)}) collective-permute-start(bf16[1,352,128]{2,1,0:T(8,128)(2,1)S(1)} %get-tuple-element.49), channel_id=1, source_target_pairs={{1,0},{2,1},{3,2},{4,3},{5,4},{6,5},{7,6},{8,7},{9,8},{10,9},{11,1... | collective-permute-start | bytes 270344 | tf_op jit(solution)/shard_map/ppermute | solution.py:22
  274.9 8.9 %copy-start.14 = (bf16[16,352,128]{2,1,0:T(8,128)(2,1)S(1)}, bf16[16,352,128]{2,1,0:T(8,128)(2,1)}, u32[]{:S(2)}) copy-start(bf16[16,352,128]{2,1,0:T(8,128)(2,1)} %param.10) | copy-start | bytes 4325380
  283.9 5.9 %copy-start.1 = (bf16[16,352,512]{2,1,0:T(8,128)(2,1)S(1)}, bf16[16,352,512]{2,1,0:T(8,128)(2,1)}, u32[]{:S(2)}) copy-start(bf16[16,352,512]{2,1,0:T(8,128)(2,1)} %copy.36) | copy-start | bytes 17301508
  283.9 5.9 %copy-start.16 = (pred[16,352,128]{2,1,0:T(32,128)(4,1)S(1)}, pred[16,352,128]{2,1,0:T(32,128)(4,1)}, u32[]{:S(2)}) copy-start(pred[16,352,128]{2,1,0:T(32,128)(4,1)} %broadcast_compare_fusion) | copy-start | bytes 2162692
  283.9 5.8 %copy-start.30 = (bf16[128,512]{1,0:T(8,128)(2,1)S(1)}, bf16[128,512]{1,0:T(8,128)(2,1)}, u32[]{:S(2)}) copy-start(bf16[128,512]{1,0:T(8,128)(2,1)} %param.15) | copy-start | bytes 393220
  300.3 5.0 %collective-permute-start = (bf16[1,352,128]{2,1,0:T(8,128)(2,1)S(1)}, bf16[1,352,128]{2,1,0:T(8,128)(2,1)S(1)}, u32[]{:S(2)}, u32[]{:S(2)}) collective-permute-start(bf16[1,352,128]{2,1,0:T(8,128)(2,1)S(1)} %get-tuple-element.52), channel_id=1, source_target_pairs={{0,1},{1,2},{2,3},{3,4},{4,5},{5,6},{6,7},{7,8},{8,9},{9,10},{10,1... | collective-permute-start | bytes 270344 | tf_op jit(solution)/shard_map/ppermute | solution.py:21
  303.0 11.0 %collective-permute-start.1 = (bf16[1,352,128]{2,1,0:T(8,128)(2,1)S(1)}, bf16[1,352,128]{2,1,0:T(8,128)(2,1)S(1)}, u32[]{:S(2)}, u32[]{:S(2)}) collective-permute-start(bf16[1,352,128]{2,1,0:T(8,128)(2,1)S(1)} %get-tuple-element.53), channel_id=1, source_target_pairs={{1,0},{2,1},{3,2},{4,3},{5,4},{6,5},{7,6},{8,7},{9,8},{10,9},{11,1... | collective-permute-start | bytes 270344 | tf_op jit(solution)/shard_map/ppermute | solution.py:22
  305.2 183.5 %reduce-scatter.4.cloned.1.call-start = ((), (), s32[]{:S(2)}) async-start(), calls=%async_computation.2 | async-start | bytes 278528
  (16 other events, 30.9 us)
Sparse Core Ops, SparseCore 0:
  305.3 124.6 all-reduce.4
  433.5 55.1 reduce-scatter.3
